TPU v7x, 32 devices: a whole 2x2x4 slice. The times are simulated.
32 devices in a mesh: freq: 8 (over z, x), unk: 4 (over y, core).
Axes of the slice: x: 2, y: 2, z: 4, core: 2. Of those that a mesh axis runs over, the one named last changes fastest.
Arguments:
- time_samples: bfloat16 [16, 32, 2048], P(None, 'freq', 'unk'), may hold values from -3 to 3
- inverse_offset: bfloat16 [2, 8, 2048, 512], P(None, 'freq', 'unk'), may hold values from -0.09375 to 0.09375
- coupling_near: bfloat16 [2, 8, 2048, 512], P(None, 'freq', 'unk'), may hold values from -0.125 to 0.125
- coupling_far: bfloat16 [2, 8, 2048, 512], P(None, 'freq', 'unk'), may hold values from -0.09375 to 0.09375
Outputs:
- solution: bfloat16 [2, 8, 32, 2048], P(None, 'freq', None, 'unk')
All inputs are finite; a program needn't handle non-finite values.
Results may differ from a plain program's by a relative error of at most 0.017.
Values may be sent and summed in bfloat16 or wider, within the bound.
A program may use at most 64 MiB of HBM per device.

v0:
```python
import math

import jax
import jax.numpy as jnp
from jax import lax
from jax.sharding import PartitionSpec as P


def from_behind(value, axis, steps):
    count = lax.axis_size(axis)
    leading, last = (max(0, -steps), min(count, count - steps))
    return lax.ppermute(value, axis, [(source, source + steps) for source in range(leading, last)])


def complex_product(factor_one, factor_two):
    real_part = jnp.einsum(
        "fmk,fkn->fmn", factor_one[0], factor_two[0], preferred_element_type=jnp.float32
    ) - jnp.einsum("fmk,fkn->fmn", factor_one[1], factor_two[1], preferred_element_type=jnp.float32)
    imag_part = jnp.einsum(
        "fmk,fkn->fmn", factor_one[0], factor_two[1], preferred_element_type=jnp.float32
    ) + jnp.einsum("fmk,fkn->fmn", factor_one[1], factor_two[0], preferred_element_type=jnp.float32)
    return jnp.stack([real_part, imag_part])


def transform_table(time_count, freq_count):
    moment = jnp.arange(time_count, dtype=jnp.int32)
    harmonic = jnp.arange(freq_count, dtype=jnp.int32)
    phase_angle = (harmonic[:, None] * moment[None, :] % time_count).astype(jnp.float32) * (
        2.0 * math.pi / time_count
    )
    damping = jnp.power(0.5, moment.astype(jnp.float32) / time_count) / math.sqrt(time_count)
    return jnp.stack([damping * jnp.cos(phase_angle), -damping * jnp.sin(phase_angle)])


def solve_step(driven_part, previous, before_previous, near_reduced, far_reduced):
    fresh_block = (
        driven_part
        - complex_product(previous, near_reduced)
        - complex_product(before_previous, far_reduced)
    )
    return fresh_block.astype(jnp.bfloat16)


def sweep(driven, near_reduced, far_reduced, group_count, forward):
    position = lax.axis_index("unk")
    devices = lax.axis_size("unk")
    load_count = driven.shape[2]
    group_width = load_count // group_count
    blank_block = jnp.zeros((2, driven.shape[1], group_width, driven.shape[3]), jnp.bfloat16)
    solved = jnp.zeros(driven.shape, jnp.bfloat16)

    def turn(turn_index, loop_state):
        solved_now, previous, before_previous = loop_state
        group = turn_index - position
        active = jnp.logical_and(group >= 0, group < group_count)
        fresh_block = lax.cond(
            active,
            lambda: solve_step(driven, previous, before_previous, near_reduced, far_reduced),
            lambda: blank_block,
        )
        stored_part = solved_now
        solved_now = jnp.where(active, fresh_block, stored_part)
        received, received_before = forward(fresh_block, previous)
        return (solved_now, received, received_before)

    final_state = lax.fori_loop(
        0, devices + group_count - 1, turn, (solved, blank_block, blank_block)
    )
    return final_state[0]


def per_device(time_samples, inverse_offset, coupling_near, coupling_far):
    time_count = time_samples.shape[0]
    weights_table = transform_table(time_count, time_count // 2)
    local_spectra = jnp.einsum(
        "ckt,tln->ckln",
        weights_table,
        time_samples.astype(jnp.float32),
        precision=lax.Precision.HIGHEST,
    ).astype(jnp.bfloat16)
    spectra = lax.all_to_all(local_spectra, "freq", split_axis=1, concat_axis=2, tiled=True)
    near_reduced = (
        coupling_near.astype(jnp.float32) + complex_product(coupling_near, inverse_offset)
    ).astype(jnp.bfloat16)
    far_reduced = (
        coupling_far.astype(jnp.float32) + complex_product(coupling_far, inverse_offset)
    ).astype(jnp.bfloat16)
    driven = spectra.astype(jnp.float32) + complex_product(spectra, inverse_offset)

    def forward_whole(fresh_block, previous):
        return from_behind((fresh_block, previous), "unk", 1)

    solution = sweep(driven, near_reduced, far_reduced, 1, forward_whole)
    return solution


def solution(mesh):
    placed = (
        P(None, "freq", "unk"),
        P(None, "freq", "unk", None),
        P(None, "freq", "unk", None),
        P(None, "freq", "unk", None),
    )
    return jax.shard_map(
        per_device,
        mesh=mesh,
        in_specs=placed,
        out_specs=P(None, "freq", None, "unk"),
        check_vma=False,
    )
```

profile of v0, /device:TPU:0, one launch (start us, length us, event | category | flops | bytes accessed | tf_op | source)
XLA Modules:
  0.0 58.5 jit_solution(11013767941844695242)
XLA Ops:
  0.0 0.1 sine_multiply_fusion
  0.1 1.0 %convolution_convert_fusion = bf16[2,8,4,512]{3,1,2,0:T(8,128)(2,1)S(1)} fusion(bf16[16,4,512]{2,1,0:T(4,128)(2,1)} %param.8, f32[1,8,16]{2,1,0:T(8,128)S(1)} %get-tuple-element.212, f32[1,8,16]{2,1,0:T(8,128)S(1)} %get-tuple-element.213), kind=kOutput, calls=%fused_computation.60 | convolution fusion | flops 6324480 | bytes 132096 | tf_op jit(solution)/shard_map/ckt,tln->ckln/dot_general | solution.py:75
  1.1 0.7 %copy.16 = bf16[2,8,4,512]{3,2,0,1:T(4,128)(2,1)} copy(bf16[2,8,4,512]{3,1,2,0:T(8,128)(2,1)S(1)} %convolution_convert_fusion) | data formatting | bytes 131072 | tf_op jit(solution)/shard_map/convert_element_type | solution.py:80
  1.8 7.3 %all-to-all-start = ((bf16[2,8,4,512]{3,2,0,1:T(4,128)(2,1)}), bf16[2,8,4,512]{3,2,0,1:T(4,128)(2,1)S(1)}, u32[]{:S(2)}, u32[]{:S(2)}) async-start(bf16[2,8,4,512]{3,2,0,1:T(4,128)(2,1)} %copy.16), calls=%async_computation | async-start | bytes 131072 | tf_op jit(solution)/shard_map/all_to_all | solution.py:81
  9.1 1.8 %fusion.52 = f32[512,512]{1,0:T(8,128)S(1)} fusion(bf16[2,1,512,512]{3,2,1,0:T(8,128)(2,1)} %param.11, bf16[2,1,512,512]{3,2,1,0:T(8,128)(2,1)} %param.9), kind=kOutput, calls=%fused_computation.67 | convolution fusion | flops 268435456 | bytes 2097152 | tf_op jit(solution)/shard_map/fmk,fkn->fmn/dot_general | solution.py:19
  10.9 0.0 copy-done.2
  10.9 0.4 fusion.54
  11.4 0.8 %copy-done.1 = bf16[2,1,512,512]{3,2,1,0:T(8,128)(2,1)S(1)} copy-done((bf16[2,1,512,512]{3,2,1,0:T(8,128)(2,1)S(1)}, bf16[2,1,512,512]{3,2,1,0:T(8,128)(2,1)}, u32[]{:S(2)}) %copy-start.1) | copy-done | bytes 1048600
  12.1 0.4 fusion.61
  12.6 0.4 fusion.72
  13.0 0.4 fusion.44
  13.5 0.4 fusion.45
  13.9 0.4 fusion.46
  14.3 0.4 fusion.47
  14.8 0.7 %fusion.42 = (bf16[2,1,512,512]{3,2,1,0:T(8,128)(2,1)S(1)}, bf16[2,1,512,512]{3,2,1,0:T(8,128)(2,1)S(1)}) fusion(f32[1,1,512,512]{3,2,1,0:T(8,128)S(1)} %fusion.46, f32[1,1,512,512]{3,2,1,0:T(8,128)S(1)} %fusion.47, bf16[2,1,512,512]{3,2,1,0:T(8,128)(2,1)S(1)} %copy-done.1, f32[1,1,512,512]{3,2,1,0:T(8,128)S(1)} %fusion.44, ...), kind=kLoop, calls=%fused_computation.49 | loop fusion | flops 4194304 | bytes 8388608 | tf_op jit(solution)/shard_map/convert_element_type | solution.py:84
  15.5 0.4 all-to-all-done
  16.0 0.2 fusion.58
  16.2 0.2 fusion.69
  16.4 0.2 fusion.48
  16.6 0.2 fusion.49
  16.9 0.1 copy.18
  17.0 40.8 %while.18 = (s32[]{:T(128)}, bf16[2,1,32,512]{3,2,1,0:T(8,128)(2,1)S(1)}, bf16[2,1,32,512]{3,2,1,0:T(8,128)(2,1)S(1)}, bf16[2,1,32,512]{3,2,1,0:T(8,128)(2,1)S(1...) while((s32[]{:T(128)}, ...), condition=%wide.region_3.4_spmd.clone, body=%wide.region_0.3_spmd.clone.sunk | while | flops 134512640 | bytes 6684950 | solution.py:66
  17.1 0.6 %copy.35 = bf16[2,1,32,512]{3,2,1,0:T(8,128)(2,1)} copy(bf16[2,1,32,512]{3,2,1,0:T(8,128)(2,1)S(1)} %get-tuple-element.277) | data formatting | bytes 131072 | tf_op jit(solution)/shard_map/while
  17.7 1.3 %collective-permute-start.1 = (bf16[2,1,32,512]{3,2,1,0:T(8,128)(2,1)}, bf16[2,1,32,512]{3,2,1,0:T(8,128)(2,1)S(1)}, u32[]{:S(2)}, u32[]{:S(2)}) collective-permute-start(bf16[2,1,32,512]{3,2,1,0:T(8,128)(2,1)} %copy.35), channel_id=1, source_target_pairs={{0,1},{1,2},{2,3},{4,5},{5,6},{6,7},{8,9},{9,10},{10,11},{12,13},{... | collective-permute-start | bytes 196616 | tf_op jit(solution)/shard_map/while/body/eval_jaxpr/ppermute | solution.py:12
  19.0 4.7 %conditional.3 = (bf16[2,1,32,512]{3,2,1,0:T(8,128)(2,1)S(1)}) conditional(s32[]{:T(128)} %convert_element_type.97, () %tuple.45, (bf16[2,1,32,512]{3,2,1,0:T(8,128)(2,1)}, bf16[2,1,512,512]{3,2,1,0:T(8,128)(2,1)S(1)}, f32[2,1,32,512]{3,2,1,0:T(8,128)S(1)}, bf16[2,1,32,512]{3,2,1,0:T(8,128)(2,1)S(1)}, bf16[2,1,512,512]{3,2,1,0:T(8,128)(2,1)S(1)}) %tuple.46), branch_computations={%region_1.1_spmd, %region_2.2_spmd} | conditional | flops 134447104 | bytes 5701640 | solution.py:56
  19.0 0.2 fusion.4
  19.2 0.2 fusion
  19.4 0.2 fusion.8
  19.6 0.2 fusion.1
  19.8 1.0 %fusion.10 = f32[32,512]{1,0:T(8,128)S(1)} fusion(bf16[2,1,512,512]{3,2,1,0:T(8,128)(2,1)S(1)} %get-tuple-element.153, bf16[2,1,32,512]{3,2,1,0:T(8,128)(2,1)} %get-tuple-element.152), kind=kOutput, calls=%fused_computation.14 | convolution fusion | flops 16777216 | bytes 622592 | tf_op jit(solution)/shard_map/while/body/eval_jaxpr/cond/branch_1_fun/fmk,fkn->fmn/dot_general | solution.py:19
  20.8 1.0 %fusion.2 = f32[1,1,32,512]{3,2,1,0:T(8,128)S(1)} fusion(f32[32,512]{1,0:T(8,128)S(1)} %fusion.10, bf16[2,1,512,512]{3,2,1,0:T(8,128)(2,1)S(1)} %get-tuple-element.153, bf16[2,1,32,512]{3,2,1,0:T(8,128)(2,1)} %get-tuple-element.152), kind=kOutput, calls=%fused_computation.5 | convolution fusion | flops 16793600 | bytes 688128 | tf_op jit(solution)/shard_map/while/body/eval_jaxpr/cond/branch_1_fun/fmk,fkn->fmn/dot_general | solution.py:21
  21.7 1.0 %fusion.14 = f32[32,512]{1,0:T(8,128)S(1)} fusion(bf16[2,1,512,512]{3,2,1,0:T(8,128)(2,1)S(1)} %get-tuple-element.153, bf16[2,1,32,512]{3,2,1,0:T(8,128)(2,1)} %get-tuple-element.152), kind=kOutput, calls=%fused_computation.18 | convolution fusion | flops 16777216 | bytes 622592 | tf_op jit(solution)/shard_map/while/body/eval_jaxpr/cond/branch_1_fun/fmk,fkn->fmn/dot_general | solution.py:16
  22.7 1.0 %fusion.3 = f32[1,1,32,512]{3,2,1,0:T(8,128)S(1)} fusion(f32[32,512]{1,0:T(8,128)S(1)} %fusion.14, bf16[2,1,512,512]{3,2,1,0:T(8,128)(2,1)S(1)} %get-tuple-element.153, bf16[2,1,32,512]{3,2,1,0:T(8,128)(2,1)} %get-tuple-element.152), kind=kOutput, calls=%fused_computation.7 | convolution fusion | flops 16793600 | bytes 688128 | tf_op jit(solution)/shard_map/while/body/eval_jaxpr/cond/branch_1_fun/fmk,fkn->fmn/dot_general | solution.py:18
  23.7 1.3 %collective-permute-start = (bf16[2,1,32,512]{3,2,1,0:T(8,128)(2,1)S(1)}, bf16[2,1,32,512]{3,2,1,0:T(8,128)(2,1)S(1)}, u32[]{:S(2)}, u32[]{:S(2)}) collective-permute-start(bf16[2,1,32,512]{3,2,1,0:T(8,128)(2,1)S(1)} %get-tuple-element.295), channel_id=1, source_target_pairs={{0,1},{1,2},{2,3},{4,5},{5,6},{6,7},{8,9},{9,10},{10,11},{12,13},{... | collective-permute-start | bytes 196616 | tf_op jit(solution)/shard_map/while/body/eval_jaxpr/ppermute | solution.py:12
  25.0 0.8 %collective-permute-done = bf16[2,1,32,512]{3,2,1,0:T(8,128)(2,1)S(1)} collective-permute-done((bf16[2,1,32,512]{3,2,1,0:T(8,128)(2,1)S(1)}, bf16[2,1,32,512]{3,2,1,0:T(8,128)(2,1)S(1)}, u32[]{:S(2)}, u32[]{:S(2)}) %collective-permute-start) | collective-permute-done | bytes 65568 | tf_op jit(solution)/shard_map/while/body/eval_jaxpr/ppermute | solution.py:12
  25.9 0.6 %copy.35 = bf16[2,1,32,512]{3,2,1,0:T(8,128)(2,1)} copy(bf16[2,1,32,512]{3,2,1,0:T(8,128)(2,1)S(1)} %get-tuple-element.277) | data formatting | bytes 131072 | tf_op jit(solution)/shard_map/while
  26.5 2.2 %collective-permute-start.1 = (bf16[2,1,32,512]{3,2,1,0:T(8,128)(2,1)}, bf16[2,1,32,512]{3,2,1,0:T(8,128)(2,1)S(1)}, u32[]{:S(2)}, u32[]{:S(2)}) collective-permute-start(bf16[2,1,32,512]{3,2,1,0:T(8,128)(2,1)} %copy.35), channel_id=1, source_target_pairs={{0,1},{1,2},{2,3},{4,5},{5,6},{6,7},{8,9},{9,10},{10,11},{12,13},{... | collective-permute-start | bytes 196616 | tf_op jit(solution)/shard_map/while/body/eval_jaxpr/ppermute | solution.py:12
  28.8 7.2 %collective-permute-start = (bf16[2,1,32,512]{3,2,1,0:T(8,128)(2,1)S(1)}, bf16[2,1,32,512]{3,2,1,0:T(8,128)(2,1)S(1)}, u32[]{:S(2)}, u32[]{:S(2)}) collective-permute-start(bf16[2,1,32,512]{3,2,1,0:T(8,128)(2,1)S(1)} %get-tuple-element.295), channel_id=1, source_target_pairs={{0,1},{1,2},{2,3},{4,5},{5,6},{6,7},{8,9},{9,10},{10,11},{12,13},{... | collective-permute-start | bytes 196616 | tf_op jit(solution)/shard_map/while/body/eval_jaxpr/ppermute | solution.py:12
  36.1 0.8 %collective-permute-done = bf16[2,1,32,512]{3,2,1,0:T(8,128)(2,1)S(1)} collective-permute-done((bf16[2,1,32,512]{3,2,1,0:T(8,128)(2,1)S(1)}, bf16[2,1,32,512]{3,2,1,0:T(8,128)(2,1)S(1)}, u32[]{:S(2)}, u32[]{:S(2)}) %collective-permute-start) | collective-permute-done | bytes 65568 | tf_op jit(solution)/shard_map/while/body/eval_jaxpr/ppermute | solution.py:12
  36.9 0.6 %copy.35 = bf16[2,1,32,512]{3,2,1,0:T(8,128)(2,1)} copy(bf16[2,1,32,512]{3,2,1,0:T(8,128)(2,1)S(1)} %get-tuple-element.277) | data formatting | bytes 131072 | tf_op jit(solution)/shard_map/while
  37.5 2.3 %collective-permute-start.1 = (bf16[2,1,32,512]{3,2,1,0:T(8,128)(2,1)}, bf16[2,1,32,512]{3,2,1,0:T(8,128)(2,1)S(1)}, u32[]{:S(2)}, u32[]{:S(2)}) collective-permute-start(bf16[2,1,32,512]{3,2,1,0:T(8,128)(2,1)} %copy.35), channel_id=1, source_target_pairs={{0,1},{1,2},{2,3},{4,5},{5,6},{6,7},{8,9},{9,10},{10,11},{12,13},{... | collective-permute-start | bytes 196616 | tf_op jit(solution)/shard_map/while/body/eval_jaxpr/ppermute | solution.py:12
  39.9 4.3 %collective-permute-start = (bf16[2,1,32,512]{3,2,1,0:T(8,128)(2,1)S(1)}, bf16[2,1,32,512]{3,2,1,0:T(8,128)(2,1)S(1)}, u32[]{:S(2)}, u32[]{:S(2)}) collective-permute-start(bf16[2,1,32,512]{3,2,1,0:T(8,128)(2,1)S(1)} %get-tuple-element.295), channel_id=1, source_target_pairs={{0,1},{1,2},{2,3},{4,5},{5,6},{6,7},{8,9},{9,10},{10,11},{12,13},{... | collective-permute-start | bytes 196616 | tf_op jit(solution)/shard_map/while/body/eval_jaxpr/ppermute | solution.py:12
  44.3 0.8 %collective-permute-done = bf16[2,1,32,512]{3,2,1,0:T(8,128)(2,1)S(1)} collective-permute-done((bf16[2,1,32,512]{3,2,1,0:T(8,128)(2,1)S(1)}, bf16[2,1,32,512]{3,2,1,0:T(8,128)(2,1)S(1)}, u32[]{:S(2)}, u32[]{:S(2)}) %collective-permute-start) | collective-permute-done | bytes 65568 | tf_op jit(solution)/shard_map/while/body/eval_jaxpr/ppermute | solution.py:12
  45.1 0.6 %copy.35 = bf16[2,1,32,512]{3,2,1,0:T(8,128)(2,1)} copy(bf16[2,1,32,512]{3,2,1,0:T(8,128)(2,1)S(1)} %get-tuple-element.277) | data formatting | bytes 131072 | tf_op jit(solution)/shard_map/while
  45.7 7.0 %collective-permute-start.1 = (bf16[2,1,32,512]{3,2,1,0:T(8,128)(2,1)}, bf16[2,1,32,512]{3,2,1,0:T(8,128)(2,1)S(1)}, u32[]{:S(2)}, u32[]{:S(2)}) collective-permute-start(bf16[2,1,32,512]{3,2,1,0:T(8,128)(2,1)} %copy.35), channel_id=1, source_target_pairs={{0,1},{1,2},{2,3},{4,5},{5,6},{6,7},{8,9},{9,10},{10,11},{12,13},{... | collective-permute-start | bytes 196616 | tf_op jit(solution)/shard_map/while/body/eval_jaxpr/ppermute | solution.py:12
  52.7 4.3 %collective-permute-start = (bf16[2,1,32,512]{3,2,1,0:T(8,128)(2,1)S(1)}, bf16[2,1,32,512]{3,2,1,0:T(8,128)(2,1)S(1)}, u32[]{:S(2)}, u32[]{:S(2)}) collective-permute-start(bf16[2,1,32,512]{3,2,1,0:T(8,128)(2,1)S(1)} %get-tuple-element.295), channel_id=1, source_target_pairs={{0,1},{1,2},{2,3},{4,5},{5,6},{6,7},{8,9},{9,10},{10,11},{12,13},{... | collective-permute-start | bytes 196616 | tf_op jit(solution)/shard_map/while/body/eval_jaxpr/ppermute | solution.py:12
  57.1 0.8 %collective-permute-done = bf16[2,1,32,512]{3,2,1,0:T(8,128)(2,1)S(1)} collective-permute-done((bf16[2,1,32,512]{3,2,1,0:T(8,128)(2,1)S(1)}, bf16[2,1,32,512]{3,2,1,0:T(8,128)(2,1)S(1)}, u32[]{:S(2)}, u32[]{:S(2)}) %collective-permute-start) | collective-permute-done | bytes 65568 | tf_op jit(solution)/shard_map/while/body/eval_jaxpr/ppermute | solution.py:12
  57.9 0.6 %copy-done.3 = bf16[2,1,32,512]{3,2,1,0:T(8,128)(2,1)} copy-done((bf16[2,1,32,512]{3,2,1,0:T(8,128)(2,1)}, bf16[2,1,32,512]{3,2,1,0:T(8,128)(2,1)S(1)}, u32[]{:S(2)}) %copy-start.3) | copy-done | bytes 65560
  (34 shorter events, 0.5 us)
Async XLA Ops:
  1.8 14.2 %all-to-all-start = ((bf16[2,8,4,512]{3,2,0,1:T(4,128)(2,1)}), bf16[2,8,4,512]{3,2,0,1:T(4,128)(2,1)S(1)}, u32[]{:S(2)}, u32[]{:S(2)}) async-start(bf16[2,8,4,512]{3,2,0,1:T(4,128)(2,1)} %copy.16), calls=%async_computation | async-start | bytes 131072 | tf_op jit(solution)/shard_map/all_to_all | solution.py:81
  9.1 1.8 %copy-start = (bf16[2,1,512,512]{3,2,1,0:T(8,128)(2,1)S(1)}, bf16[2,1,512,512]{3,2,1,0:T(8,128)(2,1)}, u32[]{:S(2)}) copy-start(bf16[2,1,512,512]{3,2,1,0:T(8,128)(2,1)} %param.9) | copy-start | bytes 3145732
  9.1 1.9 %copy-start.2 = (bf16[2,1,512,512]{3,2,1,0:T(8,128)(2,1)S(1)}, bf16[2,1,512,512]{3,2,1,0:T(8,128)(2,1)}, u32[]{:S(2)}) copy-start(bf16[2,1,512,512]{3,2,1,0:T(8,128)(2,1)} %param.11) | copy-start | bytes 3145732
  10.9 1.2 %copy-start.1 = (bf16[2,1,512,512]{3,2,1,0:T(8,128)(2,1)S(1)}, bf16[2,1,512,512]{3,2,1,0:T(8,128)(2,1)}, u32[]{:S(2)}) copy-start(bf16[2,1,512,512]{3,2,1,0:T(8,128)(2,1)} %param.10) | copy-start | bytes 3145732
  17.7 7.3 %collective-permute-start.1 = (bf16[2,1,32,512]{3,2,1,0:T(8,128)(2,1)}, bf16[2,1,32,512]{3,2,1,0:T(8,128)(2,1)S(1)}, u32[]{:S(2)}, u32[]{:S(2)}) collective-permute-start(bf16[2,1,32,512]{3,2,1,0:T(8,128)(2,1)} %copy.35), channel_id=1, source_target_pairs={{0,1},{1,2},{2,3},{4,5},{5,6},{6,7},{8,9},{9,10},{10,11},{12,13},{... | collective-permute-start | bytes 196616 | tf_op jit(solution)/shard_map/while/body/eval_jaxpr/ppermute | solution.py:12
  23.7 2.2 %collective-permute-start = (bf16[2,1,32,512]{3,2,1,0:T(8,128)(2,1)S(1)}, bf16[2,1,32,512]{3,2,1,0:T(8,128)(2,1)S(1)}, u32[]{:S(2)}, u32[]{:S(2)}) collective-permute-start(bf16[2,1,32,512]{3,2,1,0:T(8,128)(2,1)S(1)} %get-tuple-element.295), channel_id=1, source_target_pairs={{0,1},{1,2},{2,3},{4,5},{5,6},{6,7},{8,9},{9,10},{10,11},{12,13},{... | collective-permute-start | bytes 196616 | tf_op jit(solution)/shard_map/while/body/eval_jaxpr/ppermute | solution.py:12
  26.5 9.6 %collective-permute-start.1 = (bf16[2,1,32,512]{3,2,1,0:T(8,128)(2,1)}, bf16[2,1,32,512]{3,2,1,0:T(8,128)(2,1)S(1)}, u32[]{:S(2)}, u32[]{:S(2)}) collective-permute-start(bf16[2,1,32,512]{3,2,1,0:T(8,128)(2,1)} %copy.35), channel_id=1, source_target_pairs={{0,1},{1,2},{2,3},{4,5},{5,6},{6,7},{8,9},{9,10},{10,11},{12,13},{... | collective-permute-start | bytes 196616 | tf_op jit(solution)/shard_map/while/body/eval_jaxpr/ppermute | solution.py:12
  28.8 8.1 %collective-permute-start = (bf16[2,1,32,512]{3,2,1,0:T(8,128)(2,1)S(1)}, bf16[2,1,32,512]{3,2,1,0:T(8,128)(2,1)S(1)}, u32[]{:S(2)}, u32[]{:S(2)}) collective-permute-start(bf16[2,1,32,512]{3,2,1,0:T(8,128)(2,1)S(1)} %get-tuple-element.295), channel_id=1, source_target_pairs={{0,1},{1,2},{2,3},{4,5},{5,6},{6,7},{8,9},{9,10},{10,11},{12,13},{... | collective-permute-start | bytes 196616 | tf_op jit(solution)/shard_map/while/body/eval_jaxpr/ppermute | solution.py:12
  37.5 6.7 %collective-permute-start.1 = (bf16[2,1,32,512]{3,2,1,0:T(8,128)(2,1)}, bf16[2,1,32,512]{3,2,1,0:T(8,128)(2,1)S(1)}, u32[]{:S(2)}, u32[]{:S(2)}) collective-permute-start(bf16[2,1,32,512]{3,2,1,0:T(8,128)(2,1)} %copy.35), channel_id=1, source_target_pairs={{0,1},{1,2},{2,3},{4,5},{5,6},{6,7},{8,9},{9,10},{10,11},{12,13},{... | collective-permute-start | bytes 196616 | tf_op jit(solution)/shard_map/while/body/eval_jaxpr/ppermute | solution.py:12
  39.9 5.2 %collective-permute-start = (bf16[2,1,32,512]{3,2,1,0:T(8,128)(2,1)S(1)}, bf16[2,1,32,512]{3,2,1,0:T(8,128)(2,1)S(1)}, u32[]{:S(2)}, u32[]{:S(2)}) collective-permute-start(bf16[2,1,32,512]{3,2,1,0:T(8,128)(2,1)S(1)} %get-tuple-element.295), channel_id=1, source_target_pairs={{0,1},{1,2},{2,3},{4,5},{5,6},{6,7},{8,9},{9,10},{10,11},{12,13},{... | collective-permute-start | bytes 196616 | tf_op jit(solution)/shard_map/while/body/eval_jaxpr/ppermute | solution.py:12
  45.7 11.4 %collective-permute-start.1 = (bf16[2,1,32,512]{3,2,1,0:T(8,128)(2,1)}, bf16[2,1,32,512]{3,2,1,0:T(8,128)(2,1)S(1)}, u32[]{:S(2)}, u32[]{:S(2)}) collective-permute-start(bf16[2,1,32,512]{3,2,1,0:T(8,128)(2,1)} %copy.35), channel_id=1, source_target_pairs={{0,1},{1,2},{2,3},{4,5},{5,6},{6,7},{8,9},{9,10},{10,11},{12,13},{... | collective-permute-start | bytes 196616 | tf_op jit(solution)/shard_map/while/body/eval_jaxpr/ppermute | solution.py:12
  52.7 5.2 %collective-permute-start = (bf16[2,1,32,512]{3,2,1,0:T(8,128)(2,1)S(1)}, bf16[2,1,32,512]{3,2,1,0:T(8,128)(2,1)S(1)}, u32[]{:S(2)}, u32[]{:S(2)}) collective-permute-start(bf16[2,1,32,512]{3,2,1,0:T(8,128)(2,1)S(1)} %get-tuple-element.295), channel_id=1, source_target_pairs={{0,1},{1,2},{2,3},{4,5},{5,6},{6,7},{8,9},{9,10},{10,11},{12,13},{... | collective-permute-start | bytes 196616 | tf_op jit(solution)/shard_map/while/body/eval_jaxpr/ppermute | solution.py:12
  57.9 0.6 %copy-start.3 = (bf16[2,1,32,512]{3,2,1,0:T(8,128)(2,1)}, bf16[2,1,32,512]{3,2,1,0:T(8,128)(2,1)S(1)}, u32[]{:S(2)}) copy-start(bf16[2,1,32,512]{3,2,1,0:T(8,128)(2,1)S(1)} %get-tuple-element.298) | copy-start | bytes 196612
where the time goes:
time: 59.3 us; the launch traced here: 58.5 us
  starting transfers between devices  37.2 us (63%)
  matrix products  11.2 us (19%)
  local copies, waits for them, and re-layouts  4.89 us (8%)
  waiting for transfers between devices  3.7 us (6%)
  other arithmetic  1.03 us (2%)
    ppermute x8, starting transfers between devices, from_behind(): lax.ppermute(value, axis, [(source, source + steps) for source in range(l...  29.9 us
    all_to_all x1, starting transfers between devices, per_device(): lax.all_to_all(local_spectra, 'freq', split_axis=1, concat_axis=2, tiled=...  7.28 us
    dot_general x5, matrix products, complex_product(): jnp.einsum('fmk,fkn->fmn', factor_one[0], factor_two[1], preferred_elemen...  3.53 us
    ppermute x8, waiting for transfers between devices, from_behind(): lax.ppermute(value, axis, [(source, source + steps) for source in range(l...  3.26 us
    while x8, local copies, waits for them, and re-layouts  2.54 us
    dot_general x5, matrix products, complex_product(): jnp.einsum('fmk,fkn->fmn', factor_one[1], factor_two[1], preferred_elemen...  2.23 us
    dot_general x5, matrix products, complex_product(): jnp.einsum('fmk,fkn->fmn', factor_one[0], factor_two[0], preferred_elemen...  2.22 us
    dot_general x5, matrix products, complex_product(): jnp.einsum('fmk,fkn->fmn', factor_one[1], factor_two[0], preferred_elemen...  2.21 us
  transfers between devices with their start and end apart: 9, of which 5 were waited for; matrix products, arithmetic and copies ran while one was open for 18% of the time, Pallas kernels for 0%

commit v1 on v0

v1 whole, which is shorter than its diff:
```python
import functools
import math

import jax
import jax.numpy as jnp
import numpy as np
from jax import lax
from jax.experimental import pallas as pl
from jax.experimental.pallas import tpu as pltpu
from jax.sharding import PartitionSpec as P

MESH = pl.DeviceIdType.MESH


def transform_matrix(times, freqs, loads):
    moment = np.arange(times)
    angle = (np.arange(freqs)[:, None] * moment[None, :] % times) * (2.0 * math.pi / times)
    damping = np.power(0.5, moment / times) / math.sqrt(times)
    table = np.stack([damping * np.cos(angle), -damping * np.sin(angle)], axis=1)
    full = np.einsum("kct,lm->kcltm", table, np.eye(loads)).astype(np.float32)
    full = full.reshape(freqs * 2 * loads, times * loads)
    high = full.astype(jnp.bfloat16)
    rest = (full - high.astype(np.float32)).astype(jnp.bfloat16)
    return np.concatenate([high, rest], axis=1)


def dot(left, right):
    return jnp.dot(left, right, preferred_element_type=jnp.float32)


def widened(value):
    half = value.shape[0] // 2
    real, imag = value[:half], value[half:]
    return jnp.concatenate(
        [jnp.concatenate([real, -imag], axis=1), jnp.concatenate([imag, real], axis=1)], axis=0
    )


def kernel(
    n_freq, n_unk, chunk,
    ts_hbm, w_hbm, o_hbm, c_hbm, f_hbm, out_ref,
    ts, w, o, c, f, near, far, sp, rb, xb, xin, acc,
    load_sem, send_sem, recv_sem, xsend_sem, xrecv_sem,
):
    me = lax.axis_index("freq")
    pos = lax.axis_index("unk")
    loads = ts.shape[1]
    rows = o.shape[1]

    copies = [
        pltpu.make_async_copy(src, dst, load_sem.at[i])
        for i, (src, dst) in enumerate(
            [(ts_hbm, ts), (w_hbm, w), (o_hbm.at[:, 0], o), (c_hbm.at[:, 0], c), (f_hbm.at[:, 0], f)]
        )
    ]
    for copy in copies:
        copy.start()

    barrier = pltpu.get_barrier_semaphore()
    for d in range(1, n_freq):
        pl.semaphore_signal(
            barrier, inc=1, device_id={"freq": lax.rem(me + d, n_freq)}, device_id_type=MESH
        )
    for d in (1, 2):
        @pl.when(pos + d < n_unk)
        def _():
            pl.semaphore_signal(barrier, inc=1, device_id={"unk": pos + d}, device_id_type=MESH)

        @pl.when(pos >= d)
        def _():
            pl.semaphore_signal(barrier, inc=1, device_id={"unk": pos - d}, device_id_type=MESH)

    copies[0].wait()
    copies[1].wait()
    samples = ts[...].astype(jnp.float32).reshape(-1, rows).astype(jnp.bfloat16)
    spectra = dot(w[...], jnp.concatenate([samples, samples], axis=0))
    sp[...] = spectra.reshape(sp.shape).astype(jnp.bfloat16)

    def reduce_block(src, dst):
        def part(i):
            at = pl.ds(pl.multiple_of(i * chunk, chunk), chunk)
            real, imag = src[0, at, :], src[1, at, :]
            weights = o[...].reshape(2 * rows, rows)
            new_real = dot(jnp.concatenate([real, -imag], axis=1), weights)
            dst[0, at, :] = (real.astype(jnp.float32) + new_real).astype(jnp.bfloat16)
            new_imag = dot(jnp.concatenate([imag, real], axis=1), weights)
            dst[1, at, :] = (imag.astype(jnp.float32) + new_imag).astype(jnp.bfloat16)

        pl.loop(0, rows // chunk)(part)

    copies[2].wait()
    copies[3].wait()
    copies[4].wait()

    pl.semaphore_wait(
        barrier,
        n_freq - 1
        + sum(
            (pos + d < n_unk).astype(jnp.int32) + (pos >= d).astype(jnp.int32) for d in (1, 2)
        ),
    )

    sends = []
    for d in range(1, n_freq):
        target = lax.rem(me + d, n_freq)
        send = pltpu.make_async_remote_copy(
            src_ref=sp.at[target], dst_ref=rb.at[me],
            send_sem=send_sem.at[d], recv_sem=recv_sem.at[me],
            device_id={"freq": target}, device_id_type=MESH,
        )
        send.start()
        sends.append(send)
    rb[me] = sp[me]

    @pl.when(pos >= 1)
    def _():
        reduce_block(c, near)

    @pl.when(pos >= 2)
    def _():
        reduce_block(f, far)

    for d in range(1, n_freq):
        source = lax.rem(me + n_freq - d, n_freq)
        pltpu.make_async_remote_copy(
            src_ref=rb.at[source], dst_ref=rb.at[source],
            send_sem=send_sem.at[d], recv_sem=recv_sem.at[source],
            device_id={"freq": source}, device_id_type=MESH,
        ).wait_recv()

    got = rb[...].astype(jnp.float32)
    got = jnp.concatenate(
        [got[:, :loads].reshape(-1, rows), got[:, loads:].reshape(-1, rows)], axis=0
    )
    driven = got + dot(widened(got.astype(jnp.bfloat16)), o[...].reshape(2 * rows, rows))
    acc[...] = driven

    def hop(slot, step):
        return pltpu.make_async_remote_copy(
            src_ref=xb, dst_ref=xin.at[slot],
            send_sem=xsend_sem.at[slot], recv_sem=xrecv_sem.at[slot],
            device_id={"unk": lax.rem(pos + step, n_unk)}, device_id_type=MESH,
        )

    @pl.when(pos >= 2)
    def _():
        hop(1, 2).wait_recv()
        acc[...] -= dot(widened(xin[1]), far[...].reshape(2 * rows, rows))

    @pl.when(pos >= 1)
    def _():
        hop(0, 1).wait_recv()
        acc[...] -= dot(widened(xin[0]), near[...].reshape(2 * rows, rows))

    xb[...] = acc[...].astype(jnp.bfloat16)

    @pl.when(pos + 1 < n_unk)
    def _():
        hop(0, 1).start()

    @pl.when(pos + 2 < n_unk)
    def _():
        hop(1, 2).start()

    out_ref[...] = xb[...].reshape(out_ref.shape)

    for send in sends:
        send.wait_send()

    @pl.when(pos + 1 < n_unk)
    def _():
        hop(0, 1).wait_send()

    @pl.when(pos + 2 < n_unk)
    def _():
        hop(1, 2).wait_send()


def per_device(n_freq, n_unk, time_samples, inverse_offset, coupling_near, coupling_far):
    times, loads, rows = time_samples.shape
    freqs = inverse_offset.shape[1] * n_freq
    table = jnp.asarray(transform_matrix(times, freqs, loads))
    block = (2, rows, rows)
    wide = 2 * n_freq * loads
    bf16 = jnp.bfloat16
    return pl.pallas_call(
        functools.partial(kernel, n_freq, n_unk, min(256, rows)),
        out_shape=jax.ShapeDtypeStruct((2, 1, n_freq * loads, rows), bf16),
        in_specs=[pl.BlockSpec(memory_space=pl.ANY)] * 5,
        out_specs=pl.BlockSpec(memory_space=pltpu.VMEM),
        scratch_shapes=[
            pltpu.VMEM(time_samples.shape, bf16),
            pltpu.VMEM(table.shape, bf16),
            pltpu.VMEM(block, bf16),
            pltpu.VMEM(block, bf16),
            pltpu.VMEM(block, bf16),
            pltpu.VMEM(block, bf16),
            pltpu.VMEM(block, bf16),
            pltpu.VMEM((n_freq, 2 * loads, rows), bf16),
            pltpu.VMEM((n_freq, 2 * loads, rows), bf16),
            pltpu.VMEM((wide, rows), bf16),
            pltpu.VMEM((2, wide, rows), bf16),
            pltpu.VMEM((wide, rows), jnp.float32),
            pltpu.SemaphoreType.DMA((5,)),
            pltpu.SemaphoreType.DMA((n_freq,)),
            pltpu.SemaphoreType.DMA((n_freq,)),
            pltpu.SemaphoreType.DMA((2,)),
            pltpu.SemaphoreType.DMA((2,)),
        ],
        compiler_params=pltpu.CompilerParams(collective_id=0, has_side_effects=True),
    )(time_samples, table, inverse_offset, coupling_near, coupling_far)


def solution(mesh):
    placed = (
        P(None, "freq", "unk"),
        P(None, "freq", "unk", None),
        P(None, "freq", "unk", None),
        P(None, "freq", "unk", None),
    )
    return jax.shard_map(
        functools.partial(per_device, mesh.shape["freq"], mesh.shape["unk"]),
        mesh=mesh,
        in_specs=placed,
        out_specs=P(None, "freq", None, "unk"),
        check_vma=False,
    )
```

time: 59.3 us -> 16.5 us (0.28)
  the two profiles are of different devices: /device:TPU:0 before, /device:TPU:5 now
where the time goes in v1:
time: 16.5 us; the launch traced here: 16.4 us
  Pallas kernels  14.9 us (90%)
  local copies, waits for them, and re-layouts  1.47 us (9%)
    pallas_call x1, Pallas kernels, per_device(): pl.pallas_call(functools.partial(kernel, n_freq, n_unk, min(256, rows)),...  14.9 us
    unnamed x1, local copies, waits for them, and re-layouts  1.47 us

profile of v1, /device:TPU:5, one launch (start us, length us, event | category | flops | bytes accessed | tf_op | source)
XLA Modules:
  0.0 16.4 jit_solution(5495027181205793976)
XLA Ops:
  0.0 14.9 %shard_map.55 = bf16[2,1,32,512]{3,2,1,0:T(8,128)(2,1)} custom-call(bf16[16,4,512]{2,1,0:T(4,128)(2,1)} %ts_hbm.1, bf16[64,128]{1,0:T(8,128)(2,1)} %constant.2.clone.w_hbm, bf16[2,1,512,512]{3,2,1,0:T(8,128)(2,1)} %o_hbm.1, bf16[2,1,512,512]{3,2,1,0:T(8,128)(2,1)} %c_hbm.1, bf16[2,1,512,512]{3,2,1,0:T(8,128)(2,1)} %f_hbm.1), custom_call_target="tpu_custom_call" | custom-call | tf_op jit(solution)/shard_map/pallas_call | solution.py:186
  14.9 1.5 %copy.7 = bf16[2,1,32,512]{3,2,1,0:T(8,128)(2,1)} copy(bf16[2,1,32,512]{3,2,1,0:T(8,128)(2,1)} %shard_map.55) | data formatting | bytes 131072

commit v2 on v1

--- a/solution.py
+++ b/solution.py
@@ -88,10 +88,6 @@
 
         pl.loop(0, rows // chunk)(part)
 
-    copies[2].wait()
-    copies[3].wait()
-    copies[4].wait()
-
     pl.semaphore_wait(
         barrier,
         n_freq - 1
@@ -101,8 +97,11 @@
     )
 
     sends = []
+    upper = (me * 2) // n_freq
     for d in range(1, n_freq):
-        target = lax.rem(me + d, n_freq)
+        rising = (d - 1) + (d - 1 >= me).astype(jnp.int32)
+        falling = (n_freq - d) - (n_freq - d <= me).astype(jnp.int32)
+        target = upper * rising + (1 - upper) * falling
         send = pltpu.make_async_remote_copy(
             src_ref=sp.at[target], dst_ref=rb.at[me],
             send_sem=send_sem.at[d], recv_sem=recv_sem.at[me],
@@ -111,6 +110,10 @@
         send.start()
         sends.append(send)
     rb[me] = sp[me]
+
+    copies[2].wait()
+    copies[3].wait()
+    copies[4].wait()
 
     @pl.when(pos >= 1)
     def _():
@@ -185,7 +188,7 @@
     bf16 = jnp.bfloat16
     return pl.pallas_call(
         functools.partial(kernel, n_freq, n_unk, min(256, rows)),
-        out_shape=jax.ShapeDtypeStruct((2, 1, n_freq * loads, rows), bf16),
+        out_shape=pltpu.VMEM((2, 1, n_freq * loads, rows), bf16),
         in_specs=[pl.BlockSpec(memory_space=pl.ANY)] * 5,
         out_specs=pl.BlockSpec(memory_space=pltpu.VMEM),
         scratch_shapes=[

time: 16.5 us -> 14.7 us (0.89)
  Pallas kernels: 14.9 us -> 13.9 us
  local copies, waits for them, and re-layouts: 1.47 us -> 0.63 us
    pallas_call x1, Pallas kernels: 14.9 us -> 13.9 us  [per_device(): pl.pallas_call(functools.partial(kernel, n_freq, n_unk, min(256, rows)),...]
    unnamed x1, local copies, waits for them, and re-layouts: 1.47 us -> 0.63 us
where the time goes in v2:
time: 14.7 us; the launch traced here: 14.6 us
  Pallas kernels  13.9 us (95%)
  local copies, waits for them, and re-layouts  0.63 us (4%)
    pallas_call x1, Pallas kernels, per_device(): pl.pallas_call(functools.partial(kernel, n_freq, n_unk, min(256, rows)),...  13.9 us
    unnamed x1, local copies, waits for them, and re-layouts  0.63 us

profile of v2, /device:TPU:5, one launch (start us, length us, event | category | flops | bytes accessed | tf_op | source)
XLA Modules:
  0.0 14.6 jit_solution(3327484626796348446)
XLA Ops:
  0.0 13.9 %shard_map.55 = bf16[2,1,32,512]{3,2,1,0:T(8,128)(2,1)S(1)} custom-call(bf16[16,4,512]{2,1,0:T(4,128)(2,1)} %ts_hbm.1, bf16[64,128]{1,0:T(8,128)(2,1)} %constant.2.clone.w_hbm, bf16[2,1,512,512]{3,2,1,0:T(8,128)(2,1)} %o_hbm.1, bf16[2,1,512,512]{3,2,1,0:T(8,128)(2,1)} %c_hbm.1, bf16[2,1,512,512]{3,2,1,0:T(8,128)(2,1)} %f_hbm.1), custom_call_target="tpu_custom_call" | custom-call | tf_op jit(solution)/shard_map/pallas_call | solution.py:189
  13.9 0.6 %copy.7 = bf16[2,1,32,512]{3,2,1,0:T(8,128)(2,1)} copy(bf16[2,1,32,512]{3,2,1,0:T(8,128)(2,1)S(1)} %shard_map.55) | data formatting | bytes 131072

commit v3 on v2

--- a/solution.py
+++ b/solution.py
@@ -39,8 +39,8 @@
 def kernel(
     n_freq, n_unk, chunk,
     ts_hbm, w_hbm, o_hbm, c_hbm, f_hbm, out_ref,
-    ts, w, o, c, f, near, far, sp, rb, xb, xin, acc,
-    load_sem, send_sem, recv_sem, xsend_sem, xrecv_sem,
+    ts, w, o, c, f, near, far, sp, rb, xb, xin, acc, first_o, first_rb,
+    load_sem, send_sem, recv_sem, xsend_sem, xrecv_sem, first_send_sem, first_recv_sem, share_sem,
 ):
     me = lax.axis_index("freq")
     pos = lax.axis_index("unk")
@@ -69,6 +69,14 @@
         @pl.when(pos >= d)
         def _():
             pl.semaphore_signal(barrier, inc=1, device_id={"unk": pos - d}, device_id_type=MESH)
+
+    @pl.when(pos == 1)
+    def _():
+        for d in range(1, n_freq):
+            pl.semaphore_signal(
+                barrier, inc=1,
+                device_id={"freq": lax.rem(me + d, n_freq), "unk": 0}, device_id_type=MESH,
+            )
 
     copies[0].wait()
     copies[1].wait()
@@ -90,18 +98,36 @@
 
     pl.semaphore_wait(
         barrier,
-        n_freq - 1
+        (n_freq - 1) * (1 + (pos == 0).astype(jnp.int32))
         + sum(
             (pos + d < n_unk).astype(jnp.int32) + (pos >= d).astype(jnp.int32) for d in (1, 2)
         ),
     )
 
+    def share_offset():
+        return pltpu.make_async_remote_copy(
+            src_ref=o_hbm.at[:, 0], dst_ref=first_o,
+            send_sem=share_sem.at[0], recv_sem=share_sem.at[1],
+            device_id={"unk": 1}, device_id_type=MESH,
+        )
+
+    def share_spectra(target, source, at):
+        return pltpu.make_async_remote_copy(
+            src_ref=sp.at[target], dst_ref=first_rb.at[source],
+            send_sem=first_send_sem.at[at], recv_sem=first_recv_sem.at[source],
+            device_id={"freq": target, "unk": 1}, device_id_type=MESH,
+        )
+
     sends = []
+    shares = []
     upper = (me * 2) // n_freq
     for d in range(1, n_freq):
         rising = (d - 1) + (d - 1 >= me).astype(jnp.int32)
         falling = (n_freq - d) - (n_freq - d <= me).astype(jnp.int32)
         target = upper * rising + (1 - upper) * falling
+        share = share_spectra(target, me, d)
+        shares.append(share)
+        pl.when(pos == 0)(share.start)
         send = pltpu.make_async_remote_copy(
             src_ref=sp.at[target], dst_ref=rb.at[me],
             send_sem=send_sem.at[d], recv_sem=recv_sem.at[me],
@@ -109,6 +135,13 @@
         )
         send.start()
         sends.append(send)
+    shares.append(share_spectra(me, me, 0))
+
+    @pl.when(pos == 0)
+    def _():
+        shares[-1].start()
+        share_offset().start()
+
     rb[me] = sp[me]
 
     copies[2].wait()
@@ -131,52 +164,106 @@
             device_id={"freq": source}, device_id_type=MESH,
         ).wait_recv()
 
-    got = rb[...].astype(jnp.float32)
-    got = jnp.concatenate(
-        [got[:, :loads].reshape(-1, rows), got[:, loads:].reshape(-1, rows)], axis=0
-    )
-    driven = got + dot(widened(got.astype(jnp.bfloat16)), o[...].reshape(2 * rows, rows))
-    acc[...] = driven
-
-    def hop(slot, step):
+    odd = lax.rem(pos, 2) == 1
+    ahead = lax.rem(pos + 1, n_unk)
+
+    def to_next(slot, src, sem):
         return pltpu.make_async_remote_copy(
-            src_ref=xb, dst_ref=xin.at[slot],
-            send_sem=xsend_sem.at[slot], recv_sem=xrecv_sem.at[slot],
-            device_id={"unk": lax.rem(pos + step, n_unk)}, device_id_type=MESH,
-        )
+            src_ref=src, dst_ref=xin.at[slot],
+            send_sem=xsend_sem.at[sem], recv_sem=xrecv_sem.at[slot],
+            device_id={"unk": ahead}, device_id_type=MESH,
+        )
+
+    def to_second():
+        return pltpu.make_async_remote_copy(
+            src_ref=xb, dst_ref=xin.at[1],
+            send_sem=xsend_sem.at[1], recv_sem=xrecv_sem.at[1],
+            device_id={"unk": lax.rem(pos + 2, n_unk)}, device_id_type=MESH,
+        )
+
+    def drive(spectra_in, offset):
+        got = spectra_in[...].astype(jnp.float32)
+        got = jnp.concatenate(
+            [got[:, :loads].reshape(-1, rows), got[:, loads:].reshape(-1, rows)], axis=0
+        )
+        return got + dot(widened(got.astype(jnp.bfloat16)), offset[...].reshape(2 * rows, rows))
+
+    acc[...] = drive(rb, o)
+
+    @pl.when(pos == 1)
+    def _():
+        for d in range(n_freq):
+            source = lax.rem(me + n_freq - d, n_freq)
+            share_spectra(source, source, d).wait_recv()
+        share_offset().wait_recv()
+        first = drive(first_rb, first_o).astype(jnp.bfloat16)
+        xin[0] = first
+
+        @pl.when(pos + 1 < n_unk)
+        def _():
+            to_next(1, xin.at[0], 2).start()
+
+        acc[...] -= dot(widened(first), near[...].reshape(2 * rows, rows))
+
+
+    has_next = jnp.logical_and(pos >= 1, pos + 1 < n_unk)
+    has_second = jnp.logical_and(jnp.logical_and(pos >= 2, pos + 2 < n_unk), jnp.logical_not(odd))
+    hands_on = jnp.logical_and(jnp.logical_and(pos >= 2, has_next), jnp.logical_not(odd))
 
     @pl.when(pos >= 2)
     def _():
-        hop(1, 2).wait_recv()
+        @pl.when(jnp.logical_not(odd))
+        def _():
+            to_second().wait_recv()
+
+        @pl.when(odd)
+        def _():
+            to_next(1, xin.at[0], 2).wait_recv()
+
         acc[...] -= dot(widened(xin[1]), far[...].reshape(2 * rows, rows))
 
-    @pl.when(pos >= 1)
-    def _():
-        hop(0, 1).wait_recv()
+    @pl.when(pos >= 2)
+    def _():
+        to_next(0, xb, 0).wait_recv()
+
+        @pl.when(hands_on)
+        def _():
+            to_next(1, xin.at[0], 2).start()
+
         acc[...] -= dot(widened(xin[0]), near[...].reshape(2 * rows, rows))
 
     xb[...] = acc[...].astype(jnp.bfloat16)
 
-    @pl.when(pos + 1 < n_unk)
-    def _():
-        hop(0, 1).start()
-
-    @pl.when(pos + 2 < n_unk)
-    def _():
-        hop(1, 2).start()
+    @pl.when(has_next)
+    def _():
+        to_next(0, xb, 0).start()
+
+    @pl.when(has_second)
+    def _():
+        to_second().start()
 
     out_ref[...] = xb[...].reshape(out_ref.shape)
 
     for send in sends:
         send.wait_send()
 
-    @pl.when(pos + 1 < n_unk)
-    def _():
-        hop(0, 1).wait_send()
-
-    @pl.when(pos + 2 < n_unk)
-    def _():
-        hop(1, 2).wait_send()
+    @pl.when(pos == 0)
+    def _():
+        for share in shares:
+            share.wait_send()
+        share_offset().wait_send()
+
+    @pl.when(jnp.logical_or(hands_on, jnp.logical_and(pos == 1, has_next)))
+    def _():
+        to_next(1, xin.at[0], 2).wait_send()
+
+    @pl.when(has_next)
+    def _():
+        to_next(0, xb, 0).wait_send()
+
+    @pl.when(has_second)
+    def _():
+        to_second().wait_send()
 
 
 def per_device(n_freq, n_unk, time_samples, inverse_offset, coupling_near, coupling_far):
@@ -204,10 +291,15 @@
             pltpu.VMEM((wide, rows), bf16),
             pltpu.VMEM((2, wide, rows), bf16),
             pltpu.VMEM((wide, rows), jnp.float32),
+            pltpu.VMEM(block, bf16),
+            pltpu.VMEM((n_freq, 2 * loads, rows), bf16),
             pltpu.SemaphoreType.DMA((5,)),
             pltpu.SemaphoreType.DMA((n_freq,)),
             pltpu.SemaphoreType.DMA((n_freq,)),
+            pltpu.SemaphoreType.DMA((3,)),
             pltpu.SemaphoreType.DMA((2,)),
+            pltpu.SemaphoreType.DMA((n_freq,)),
+            pltpu.SemaphoreType.DMA((n_freq,)),
             pltpu.SemaphoreType.DMA((2,)),
         ],
         compiler_params=pltpu.CompilerParams(collective_id=0, has_side_effects=True),

time: 14.7 us -> 13.9 us (0.946)
  Pallas kernels: 13.9 us -> 13.1 us
    pallas_call x1, Pallas kernels: 13.9 us -> 13.1 us  [per_device(): pl.pallas_call(functools.partial(kernel, n_freq, n_unk, min(256, rows)),...]
where the time goes in v3:
time: 13.9 us; the launch traced here: 13.7 us
  Pallas kernels  13.1 us (94%)
  local copies, waits for them, and re-layouts  0.63 us (5%)
    pallas_call x1, Pallas kernels, per_device(): pl.pallas_call(functools.partial(kernel, n_freq, n_unk, min(256, rows)),...  13.1 us
    unnamed x1, local copies, waits for them, and re-layouts  0.63 us

profile of v3, /device:TPU:5, one launch (start us, length us, event | category | flops | bytes accessed | tf_op | source)
XLA Modules:
  0.0 13.7 jit_solution(7215717444500366586)
XLA Ops:
  0.0 13.1 %shard_map.55 = bf16[2,1,32,512]{3,2,1,0:T(8,128)(2,1)S(1)} custom-call(bf16[16,4,512]{2,1,0:T(4,128)(2,1)} %ts_hbm.1, bf16[64,128]{1,0:T(8,128)(2,1)} %constant.2.clone.w_hbm, bf16[2,1,512,512]{3,2,1,0:T(8,128)(2,1)} %o_hbm.1, bf16[2,1,512,512]{3,2,1,0:T(8,128)(2,1)} %c_hbm.1, bf16[2,1,512,512]{3,2,1,0:T(8,128)(2,1)} %f_hbm.1), custom_call_target="tpu_custom_call" | custom-call | tf_op jit(solution)/shard_map/pallas_call | solution.py:276
  13.1 0.6 %copy.7 = bf16[2,1,32,512]{3,2,1,0:T(8,128)(2,1)} copy(bf16[2,1,32,512]{3,2,1,0:T(8,128)(2,1)S(1)} %shard_map.55) | data formatting | bytes 131072

commit v4 on v3

--- a/solution.py
+++ b/solution.py
@@ -118,16 +118,22 @@
             device_id={"freq": target, "unk": 1}, device_id_type=MESH,
         )
 
-    sends = []
-    shares = []
-    upper = (me * 2) // n_freq
-    for d in range(1, n_freq):
+    def other(d):
+        upper = (me * 2) // n_freq
         rising = (d - 1) + (d - 1 >= me).astype(jnp.int32)
         falling = (n_freq - d) - (n_freq - d <= me).astype(jnp.int32)
-        target = upper * rising + (1 - upper) * falling
-        share = share_spectra(target, me, d)
-        shares.append(share)
-        pl.when(pos == 0)(share.start)
+        return upper * rising + (1 - upper) * falling
+
+    @pl.when(pos == 0)
+    def _():
+        for d in range(1, n_freq):
+            share_spectra(other(d), me, d).start()
+        share_spectra(me, me, 0).start()
+        share_offset().start()
+
+    sends = []
+    for d in range(1, n_freq):
+        target = other(d)
         send = pltpu.make_async_remote_copy(
             src_ref=sp.at[target], dst_ref=rb.at[me],
             send_sem=send_sem.at[d], recv_sem=recv_sem.at[me],
@@ -135,13 +141,6 @@
         )
         send.start()
         sends.append(send)
-    shares.append(share_spectra(me, me, 0))
-
-    @pl.when(pos == 0)
-    def _():
-        shares[-1].start()
-        share_offset().start()
-
     rb[me] = sp[me]
 
     copies[2].wait()
@@ -249,8 +248,8 @@
 
     @pl.when(pos == 0)
     def _():
-        for share in shares:
-            share.wait_send()
+        for d in range(n_freq):
+            share_spectra(me, me, d).wait_send()
         share_offset().wait_send()
 
     @pl.when(jnp.logical_or(hands_on, jnp.logical_and(pos == 1, has_next)))

time: 13.9 us -> 13.9 us (level)
  no operation moved by 1% of the time
where the time goes in v4:
time: 13.9 us; the launch traced here: 13.7 us
  Pallas kernels  13.1 us (94%)
  local copies, waits for them, and re-layouts  0.63 us (5%)
    pallas_call x1, Pallas kernels, per_device(): pl.pallas_call(functools.partial(kernel, n_freq, n_unk, min(256, rows)),...  13.1 us
    unnamed x1, local copies, waits for them, and re-layouts  0.63 us

profile of v4, /device:TPU:5, one launch (start us, length us, event | category | flops | bytes accessed | tf_op | source)
XLA Modules:
  0.0 13.7 jit_solution(3865544276345567677)
XLA Ops:
  0.0 13.1 %shard_map.55 = bf16[2,1,32,512]{3,2,1,0:T(8,128)(2,1)S(1)} custom-call(bf16[16,4,512]{2,1,0:T(4,128)(2,1)} %ts_hbm.1, bf16[64,128]{1,0:T(8,128)(2,1)} %constant.2.clone.w_hbm, bf16[2,1,512,512]{3,2,1,0:T(8,128)(2,1)} %o_hbm.1, bf16[2,1,512,512]{3,2,1,0:T(8,128)(2,1)} %c_hbm.1, bf16[2,1,512,512]{3,2,1,0:T(8,128)(2,1)} %f_hbm.1), custom_call_target="tpu_custom_call" | custom-call | tf_op jit(solution)/shard_map/pallas_call | solution.py:275
  13.1 0.6 %copy.7 = bf16[2,1,32,512]{3,2,1,0:T(8,128)(2,1)} copy(bf16[2,1,32,512]{3,2,1,0:T(8,128)(2,1)S(1)} %shard_map.55) | data formatting | bytes 131072

commit v5 on v4

--- a/solution.py
+++ b/solution.py
@@ -53,7 +53,7 @@
             [(ts_hbm, ts), (w_hbm, w), (o_hbm.at[:, 0], o), (c_hbm.at[:, 0], c), (f_hbm.at[:, 0], f)]
         )
     ]
-    for copy in copies:
+    for copy in copies[:2]:
         copy.start()
 
     barrier = pltpu.get_barrier_semaphore()
@@ -77,6 +77,9 @@
                 barrier, inc=1,
                 device_id={"freq": lax.rem(me + d, n_freq), "unk": 0}, device_id_type=MESH,
             )
+
+    for copy in copies[2:]:
+        copy.start()
 
     copies[0].wait()
     copies[1].wait()
@@ -231,7 +234,9 @@
 
         acc[...] -= dot(widened(xin[0]), near[...].reshape(2 * rows, rows))
 
-    xb[...] = acc[...].astype(jnp.bfloat16)
+    solved = acc[...].astype(jnp.bfloat16)
+    xb[...] = solved
+    out_ref[...] = solved.reshape(out_ref.shape)
 
     @pl.when(has_next)
     def _():
@@ -241,7 +246,6 @@
     def _():
         to_second().start()
 
-    out_ref[...] = xb[...].reshape(out_ref.shape)
 
     for send in sends:
         send.wait_send()

time: 13.9 us -> 13.8 us (level)
  no operation moved by 1% of the time
where the time goes in v5:
time: 13.8 us; the launch traced here: 13.7 us
  Pallas kernels  13 us (94%)
  local copies, waits for them, and re-layouts  0.63 us (5%)
    pallas_call x1, Pallas kernels, per_device(): pl.pallas_call(functools.partial(kernel, n_freq, n_unk, min(256, rows)),...  13 us
    unnamed x1, local copies, waits for them, and re-layouts  0.63 us

profile of v5, /device:TPU:5, one launch (start us, length us, event | category | flops | bytes accessed | tf_op | source)
XLA Modules:
  0.0 13.7 jit_solution(8928791477344935893)
XLA Ops:
  0.0 13.0 %shard_map.55 = bf16[2,1,32,512]{3,2,1,0:T(8,128)(2,1)S(1)} custom-call(bf16[16,4,512]{2,1,0:T(4,128)(2,1)} %ts_hbm.1, bf16[64,128]{1,0:T(8,128)(2,1)} %constant.2.clone.w_hbm, bf16[2,1,512,512]{3,2,1,0:T(8,128)(2,1)} %o_hbm.1, bf16[2,1,512,512]{3,2,1,0:T(8,128)(2,1)} %c_hbm.1, bf16[2,1,512,512]{3,2,1,0:T(8,128)(2,1)} %f_hbm.1), custom_call_target="tpu_custom_call" | custom-call | tf_op jit(solution)/shard_map/pallas_call | solution.py:279
  13.1 0.6 %copy.7 = bf16[2,1,32,512]{3,2,1,0:T(8,128)(2,1)} copy(bf16[2,1,32,512]{3,2,1,0:T(8,128)(2,1)S(1)} %shard_map.55) | data formatting | bytes 131072
